TPU v7x, 32 devices: a whole 2x2x4 slice. The times are simulated.
32 devices in a mesh: grp: 2 (over core), dev: 16 (over z, y, x).
Axes of the slice: x: 2, y: 2, z: 4, core: 2. Of those that a mesh axis runs over, the one named last changes fastest.
Arguments:
- vectors: bfloat16 [32, 2, 384], P(('grp', 'dev')), may hold values from -6 to 6
- kernel: bfloat16 [32, 128, 384], P(None, ('grp', 'dev')), may hold values from -0.0546875 to 0.0546875
- sensor_slot: int32 [32], replicated, may hold values from 0 to 31, each once
- noise_var: float32 [32], P(('grp', 'dev')), may hold values from 0.1 to 1
- smoothing_rate: float32 [128], P(('grp', 'dev')), may hold values from 0.2 to 3
Outputs:
- hessian_vectors: float32 [32, 2, 384], P(('grp', 'dev'))
Inputs may be any that keep to these rules, and one draw needn't show every extreme that they name: sensor_slot is a permutation of the 32 sensors: row sensor_slot[s] of vectors, noise_var and hessian_vectors belongs to sensor s.
All inputs are finite; a program needn't handle non-finite values.
Results may differ from a plain program's by a relative error of at most 0.0011.
Values may be sent and summed in bfloat16 or wider, within the bound.
A program may use at most 64 MiB of HBM per device.

v0:
```python
import functools

import jax
import jax.numpy as jnp
from jax import lax
from jax.experimental import pallas as pl
from jax.experimental.pallas import tpu as pltpu
from jax.sharding import PartitionSpec as P

SWEEPS = 2
LANE = 128
F32 = jnp.float32
BF16 = jnp.bfloat16
MESH = pl.DeviceIdType.MESH


def iota(shape, dim):
    return lax.broadcasted_iota(jnp.int32, shape, dim)


def fold_rows(block):
    width = block.shape[1]
    rows = block.shape[0]
    while rows > 8:
        rows //= 2
        block = block[:rows] + pltpu.roll(block[rows:], width - rows, 1)
    return block


def fold_pair(low, high, step):
    width = low.shape[1]
    clear = (iota(low.shape, 0) & step) == 0
    first = jnp.where(clear, low, pltpu.roll(high, step, 0))
    second = jnp.where(clear, pltpu.roll(low, 8 - step, 0), high)
    return first + pltpu.roll(second, width - step, 1)


def spread_rows(row):
    block = jnp.broadcast_to(row, (8, row.shape[1]))
    for step in (4, 2, 1):
        block = jnp.where((iota(block.shape, 0) & step) == 0, block, pltpu.roll(block, step, 1))
    rows = 8
    while rows < LANE:
        block = jnp.concatenate([block, pltpu.roll(block, rows, 1)], axis=0)
        rows *= 2
    return block


def kernel_body(
    n_grp, n_dev, vec_ref, ker_hbm, slot_ref, noise_ref, rate_ref, out_ref,
    ker, gath, rates, halo_own, halo, scat_own, scat, kx_ref, kxt_ref,
    ker_sem, gath_send, gath_recv, rate_send, rate_recv, halo_send, halo_recv, scat_send, scat_recv,
):
    n = n_grp * n_dev
    sensors, points, nt = ker_hbm.shape
    vecs = vec_ref.shape[1]
    chunks = nt // LANE
    pieces = vecs * chunks
    grp, dev = lax.axis_index("grp"), lax.axis_index("dev")
    me = grp * n_dev + dev

    def place(rank):
        return (rank // n_dev, rank % n_dev)

    barrier = pltpu.get_barrier_semaphore()

    @pl.loop(1, n)
    def _(k):
        pl.semaphore_signal(barrier, inc=1, device_id=place((me + k) % n), device_id_type=MESH)

    ker_copy = pltpu.make_async_copy(ker_hbm, ker, ker_sem)
    ker_copy.start()
    own = vec_ref[0].astype(F32)
    own_rows = [own[v : v + 1, LANE * c : LANE * (c + 1)] for v in range(vecs) for c in range(chunks)]
    own_tile = jnp.concatenate(own_rows + [jnp.zeros((8 - pieces, LANE), F32)], axis=0)
    gath[0] = own_tile.astype(BF16)
    row_point = iota((8, LANE), 0) // vecs
    rate = jnp.zeros((8, LANE), F32)
    for a in range(points):
        rate = jnp.where(row_point == a, rate_ref[a], rate)
    rates[0] = rate
    pl.semaphore_wait(barrier, n - 1)

    @pl.loop(1, n)
    def _(k):
        pltpu.make_async_remote_copy(
            src_ref=gath.at[0], dst_ref=gath.at[k], send_sem=gath_send, recv_sem=gath_recv,
            device_id=place((me + k) % n), device_id_type=MESH,
        ).start()

    def beside(offset):
        return (grp, (dev + offset + n_dev) % n_dev)

    rate_copies = [
        pltpu.make_async_remote_copy(
            src_ref=rates.at[0], dst_ref=rates.at[1 + i], send_sem=rate_send.at[i], recv_sem=rate_recv.at[i],
            device_id=beside(offset), device_id_type=MESH,
        )
        for i, offset in enumerate((1, -1))
    ]
    for copy in rate_copies:
        copy.start()

    ker_copy.wait()
    owner = (me - iota((n, n), 0) + n) % n
    pick = (jnp.broadcast_to(slot_ref[...].reshape(1, n), (n, n)) == owner).astype(F32).astype(BF16)
    for p in range(points):
        picked = jnp.dot(pick, ker[:, p, :], preferred_element_type=F32)
        for c in range(chunks):
            part = picked[:, LANE * c : LANE * (c + 1)]
            kx_ref[n * c : n * (c + 1), LANE * p : LANE * (p + 1)] = part.astype(BF16)
    kxt_ref[...] = kx_ref[...].astype(F32).T.astype(BF16)

    group = 32
    wanted = iota((pieces * group, 8 * group), 0)
    sel = ((wanted % group) * 8 + wanted // group == iota((pieces * group, 8 * group), 1)).astype(F32).astype(BF16)
    lower = iota((LANE, LANE), 0) <= iota((LANE, LANE), 1)

    pltpu.make_async_copy(gath.at[1:n], gath.at[1:n], gath_recv).wait()
    parts = []
    for g in range(n // group):
        tiles = gath[group * g : group * (g + 1)].astype(F32).reshape(group * 8, LANE).astype(BF16)
        parts.append(jnp.dot(sel, tiles, preferred_element_type=F32).astype(BF16))

    def data(piece):
        return jnp.concatenate([part[group * piece : group * (piece + 1)] for part in parts], axis=0)

    zero = jnp.zeros((n, LANE), BF16)
    rows = [
        jnp.concatenate(
            [data(v * chunks + c + e) if c + e < chunks else zero for v in range(vecs) for e in range(chunks)], axis=1
        )
        for c in range(chunks)
    ]
    shifted = jnp.concatenate(rows, axis=0)
    leaves = []
    for p in range(points):
        products = jnp.dot(kxt_ref[LANE * p : LANE * (p + 1), :], shifted, preferred_element_type=F32)
        for v in range(vecs):
            block = products[:, nt * v : nt * (v + 1)]
            block = jnp.concatenate([jnp.where(lower, block[:, :LANE], 0.0), block[:, LANE:]], axis=1)
            leaves.append(fold_rows(block))
    step = 4
    while step:
        leaves = [fold_pair(leaves[i], leaves[i + step], step) for i in range(step)]
        step //= 2
    field = leaves[0]
    halo_own[...] = field

    offsets = (1, -1, 2, -2)
    halo_copies = [
        pltpu.make_async_remote_copy(
            src_ref=halo_own, dst_ref=halo.at[i], send_sem=halo_send.at[i], recv_sem=halo_recv.at[i],
            device_id=beside(offset), device_id_type=MESH,
        )
        for i, offset in enumerate(offsets)
    ]
    for copy in halo_copies:
        copy.start()
    for copy in rate_copies + halo_copies:
        copy.wait_recv()

    def wide(tile):
        return jnp.concatenate([tile] * chunks, axis=1)

    row = iota((8, nt), 0)

    def sweep(x, left, right, c):
        up = jnp.where(row < vecs, 0.0, pltpu.roll(x, vecs, 0))
        down = jnp.where(row >= 8 - vecs, 0.0, pltpu.roll(x, 8 - vecs, 0))
        return (x + c * (left + right + up + down)) / (1.0 + 4.0 * c)

    left1 = jnp.where(dev >= 1, halo[0], 0.0)
    right1 = jnp.where(dev < n_dev - 1, halo[1], 0.0)
    left2 = jnp.where(dev >= 2, halo[2], 0.0)
    right2 = jnp.where(dev < n_dev - 2, halo[3], 0.0)
    rate_own = wide(rate)
    centre = sweep(field, left1, right1, rate_own)
    left = jnp.where(dev >= 1, sweep(left1, left2, field, wide(rates[1])), 0.0)
    right = jnp.where(dev < n_dev - 1, sweep(right1, field, right2, wide(rates[2])), 0.0)
    smoothed = sweep(centre, left, right, rate_own)
    rounded = smoothed.astype(BF16).astype(F32)

    blocks = []
    for p in range(points):
        across = []
        for v in range(vecs):
            block = spread_rows(rounded[p * vecs + v : p * vecs + v + 1])
            upper = iota((LANE, LANE), 0) <= iota((LANE, LANE), 1)
            across += [jnp.where(upper, block[:, :LANE], 0.0), block[:, LANE:]]
        blocks.append(jnp.concatenate(across, axis=1).astype(BF16))
    lagged = jnp.concatenate(blocks, axis=0)
    sums = jnp.dot(kx_ref[...], lagged, preferred_element_type=F32)
    for v in range(vecs):
        for e in range(chunks):
            total = None
            for c in range(e + 1):
                first = nt * v + LANE * (e - c)
                term = sums[n * c : n * (c + 1), first : first + LANE]
                total = term if total is None else total + term
            scat_own[:, v * chunks + e, :] = total
    scat_own[:, pieces:, :] = jnp.zeros((n, 8 - pieces, LANE), F32)

    @pl.loop(1, n)
    def _(k):
        pltpu.make_async_remote_copy(
            src_ref=scat_own.at[k], dst_ref=scat.at[k], send_sem=scat_send, recv_sem=scat_recv,
            device_id=place((me - k + n) % n), device_id_type=MESH,
        ).start()

    acc = scat_own[0] + noise_ref[0] * own_tile
    pltpu.make_async_copy(scat.at[1:n], scat.at[1:n], scat_recv).wait()
    acc = acc + jnp.sum(scat[1:n], axis=0)
    for v in range(vecs):
        for c in range(chunks):
            out_ref[0, v : v + 1, LANE * c : LANE * (c + 1)] = acc[v * chunks + c : v * chunks + c + 1]
    for copy in rate_copies + halo_copies:
        copy.wait_send()
    pltpu.make_async_copy(gath.at[1:n], gath.at[1:n], gath_send).wait()
    pltpu.make_async_copy(scat.at[1:n], scat.at[1:n], scat_send).wait()


def solution(mesh):
    n_grp, n_dev = mesh.shape["grp"], mesh.shape["dev"]
    n = n_grp * n_dev

    def body(vectors, kernel, sensor_slot, noise_var, smoothing_rate):
        own, vecs, nt = vectors.shape
        sensors, points, _ = kernel.shape
        chunks = nt // LANE
        vmem, smem = pltpu.VMEM, pltpu.SMEM
        dma = pltpu.SemaphoreType.DMA
        return pl.pallas_call(
            functools.partial(kernel_body, n_grp, n_dev),
            out_shape=jax.ShapeDtypeStruct((own, vecs, nt), F32),
            in_specs=[
                pl.BlockSpec(memory_space=vmem),
                pl.BlockSpec(memory_space=pl.ANY),
                pl.BlockSpec(memory_space=vmem),
                pl.BlockSpec(memory_space=smem),
                pl.BlockSpec(memory_space=smem),
            ],
            out_specs=pl.BlockSpec(memory_space=vmem),
            scratch_shapes=[
                vmem((sensors, points, nt), BF16),
                vmem((n, 8, LANE), BF16),
                vmem((3, 8, LANE), F32),
                vmem((8, nt), F32),
                vmem((4, 8, nt), F32),
                vmem((n, 8, LANE), F32),
                vmem((n, 8, LANE), F32),
                vmem((chunks * n, points * LANE), BF16),
                vmem((points * LANE, chunks * n), BF16),
                dma, dma, dma, dma((2,)), dma((2,)), dma((4,)), dma((4,)), dma, dma,
            ],
            compiler_params=pltpu.CompilerParams(collective_id=0, has_side_effects=True),
        )(vectors, kernel, sensor_slot, noise_var, smoothing_rate)

    return jax.shard_map(
        body,
        mesh=mesh,
        in_specs=(
            P(("grp", "dev"), None, None),
            P(None, ("grp", "dev"), None),
            P(),
            P(("grp", "dev")),
            P(("grp", "dev")),
        ),
        out_specs=P(("grp", "dev"), None, None),
        check_vma=False,
    )
```

profile of v0, /device:TPU:0, one launch (start us, length us, event | category | flops | bytes accessed | tf_op | source)
XLA Modules:
  0.0 25.5 jit_solution(18002644189421470434)
XLA Ops:
  0.7 23.6 %shard_map.55 = f32[1,2,384]{2,1,0:T(2,128)} custom-call(bf16[1,2,384]{2,1,0:T(2,128)(2,1)} %vec_ref.1, bf16[32,4,384]{2,1,0:T(4,128)(2,1)} %ker_hbm.1, s32[32]{0:T(128)} %slot_ref.1, f32[1]{0:T(128)S(6)} %copy.7.noise_ref, f32[4]{0:T(128)} %rate_ref.1), custom_call_target="tpu_custom_call" | custom-call | tf_op jit(solution)/shard_map/pallas_call | solution.py:233
  24.2 1.3 %copy.8 = f32[1,2,384]{2,1,0:T(2,128)} copy(f32[1,2,384]{2,1,0:T(2,128)} %shard_map.55) | data formatting | bytes 6144
where the time goes:
time: 25.7 us; the launch traced here: 25.5 us
  Pallas kernels  23.6 us (92%)
  local copies, waits for them, and re-layouts  1.26 us (5%)
  between operations  0.66 us (3%)
    pallas_call x1, Pallas kernels, body(): pl.pallas_call(functools.partial(kernel_body, n_grp, n_dev), out_shape=ja...  23.6 us
    unnamed x1, local copies, waits for them, and re-layouts  1.26 us

commit v1 on v0

--- a/solution.py
+++ b/solution.py
@@ -47,29 +47,47 @@
 
 
 def kernel_body(
-    n_grp, n_dev, vec_ref, ker_hbm, slot_ref, noise_ref, rate_ref, out_ref,
-    ker, gath, rates, halo_own, halo, scat_own, scat, kx_ref, kxt_ref,
-    ker_sem, gath_send, gath_recv, rate_send, rate_recv, halo_send, halo_recv, scat_send, scat_recv,
+    n_grp, n_dev, vec_hbm, ker_hbm, slot_hbm, noise_hbm, rate_hbm, out_ref,
+    vec_ref, slot_ref, noise_ref, rate_ref,    ker, gath, rates, halo_own, halo, scat_own, scat, kx_ref, kxt_ref,
+    load_sem, ker_sem, gath_send, gath_recv, rate_send, rate_recv, halo_send, halo_recv, scat_send, scat_recv,
 ):
     n = n_grp * n_dev
     sensors, points, nt = ker_hbm.shape
-    vecs = vec_ref.shape[1]
+    vecs = vec_hbm.shape[1]
     chunks = nt // LANE
     pieces = vecs * chunks
     grp, dev = lax.axis_index("grp"), lax.axis_index("dev")
-    me = grp * n_dev + dev
-
-    def place(rank):
-        return (rank // n_dev, rank % n_dev)
-
+
+    def ahead(k):
+        return ((grp + k // n_dev) % n_grp, (dev + k % n_dev) % n_dev)
+
+    def behind(k):
+        return ((grp - k // n_dev + n_grp) % n_grp, (dev - k % n_dev + n_dev) % n_dev)
+
+    def slot_of(i):
+        q = i // n_grp
+        along = (n_dev // 2 + (1 - 2 * (q % 2)) * ((q + 1) // 2) + n_dev) % n_dev
+        return (n_grp - 1 - i % n_grp) * n_dev + along
+
+    gath[...] = jnp.zeros(gath.shape, BF16)
     barrier = pltpu.get_barrier_semaphore()
 
     @pl.loop(1, n)
     def _(k):
-        pl.semaphore_signal(barrier, inc=1, device_id=place((me + k) % n), device_id_type=MESH)
-
+        pl.semaphore_signal(barrier, inc=1, device_id=ahead(k), device_id_type=MESH)
+
+    loads = [
+        pltpu.make_async_copy(source, target, load_sem.at[i])
+        for i, (source, target) in enumerate(
+            ((vec_hbm, vec_ref), (rate_hbm, rate_ref), (slot_hbm, slot_ref), (noise_hbm, noise_ref))
+        )
+    ]
+    for load in loads:
+        load.start()
     ker_copy = pltpu.make_async_copy(ker_hbm, ker, ker_sem)
     ker_copy.start()
+    for load in loads:
+        load.wait()
     own = vec_ref[0].astype(F32)
     own_rows = [own[v : v + 1, LANE * c : LANE * (c + 1)] for v in range(vecs) for c in range(chunks)]
     own_tile = jnp.concatenate(own_rows + [jnp.zeros((8 - pieces, LANE), F32)], axis=0)
@@ -84,8 +102,8 @@
     @pl.loop(1, n)
     def _(k):
         pltpu.make_async_remote_copy(
-            src_ref=gath.at[0], dst_ref=gath.at[k], send_sem=gath_send, recv_sem=gath_recv,
-            device_id=place((me + k) % n), device_id_type=MESH,
+            src_ref=gath.at[0, :pieces], dst_ref=gath.at[k, :pieces], send_sem=gath_send, recv_sem=gath_recv,
+            device_id=ahead(k), device_id_type=MESH,
         ).start()
 
     def beside(offset):
@@ -98,11 +116,14 @@
         )
         for i, offset in enumerate((1, -1))
     ]
-    for copy in rate_copies:
-        copy.start()
+    targets = [dev < n_dev - 1, dev >= 1, dev < n_dev - 2, dev >= 2]
+    sources = [dev >= 1, dev < n_dev - 1, dev >= 2, dev < n_dev - 2]
+    for copy, target in zip(rate_copies, targets):
+        pl.when(target)(copy.start)
 
     ker_copy.wait()
-    owner = (me - iota((n, n), 0) + n) % n
+    owner_grp, owner_dev = behind(iota((n, n), 0))
+    owner = owner_grp * n_dev + owner_dev
     pick = (jnp.broadcast_to(slot_ref[...].reshape(1, n), (n, n)) == owner).astype(F32).astype(BF16)
     for p in range(points):
         picked = jnp.dot(pick, ker[:, p, :], preferred_element_type=F32)
@@ -116,7 +137,7 @@
     sel = ((wanted % group) * 8 + wanted // group == iota((pieces * group, 8 * group), 1)).astype(F32).astype(BF16)
     lower = iota((LANE, LANE), 0) <= iota((LANE, LANE), 1)
 
-    pltpu.make_async_copy(gath.at[1:n], gath.at[1:n], gath_recv).wait()
+    pltpu.make_async_copy(gath.at[1:n, :pieces], gath.at[1:n, :pieces], gath_recv).wait()
     parts = []
     for g in range(n // group):
         tiles = gath[group * g : group * (g + 1)].astype(F32).reshape(group * 8, LANE).astype(BF16)
@@ -155,10 +176,10 @@
         )
         for i, offset in enumerate(offsets)
     ]
-    for copy in halo_copies:
-        copy.start()
-    for copy in rate_copies + halo_copies:
-        copy.wait_recv()
+    for copy, target in zip(halo_copies, targets):
+        pl.when(target)(copy.start)
+    for copy, source in zip(rate_copies + halo_copies, sources[:2] + sources):
+        pl.when(source)(copy.wait_recv)
 
     def wide(tile):
         return jnp.concatenate([tile] * chunks, axis=1)
@@ -175,9 +196,11 @@
     left2 = jnp.where(dev >= 2, halo[2], 0.0)
     right2 = jnp.where(dev < n_dev - 2, halo[3], 0.0)
     rate_own = wide(rate)
+    rate_left = jnp.where(dev >= 1, rates[1], 1.0)
+    rate_right = jnp.where(dev < n_dev - 1, rates[2], 1.0)
     centre = sweep(field, left1, right1, rate_own)
-    left = jnp.where(dev >= 1, sweep(left1, left2, field, wide(rates[1])), 0.0)
-    right = jnp.where(dev < n_dev - 1, sweep(right1, field, right2, wide(rates[2])), 0.0)
+    left = jnp.where(dev >= 1, sweep(left1, left2, field, wide(rate_left)), 0.0)
+    right = jnp.where(dev < n_dev - 1, sweep(right1, field, right2, wide(rate_right)), 0.0)
     smoothed = sweep(centre, left, right, rate_own)
     rounded = smoothed.astype(BF16).astype(F32)
 
@@ -199,25 +222,24 @@
                 term = sums[n * c : n * (c + 1), first : first + LANE]
                 total = term if total is None else total + term
             scat_own[:, v * chunks + e, :] = total
-    scat_own[:, pieces:, :] = jnp.zeros((n, 8 - pieces, LANE), F32)
 
     @pl.loop(1, n)
     def _(k):
         pltpu.make_async_remote_copy(
-            src_ref=scat_own.at[k], dst_ref=scat.at[k], send_sem=scat_send, recv_sem=scat_recv,
-            device_id=place((me - k + n) % n), device_id_type=MESH,
+            src_ref=scat_own.at[k, :pieces], dst_ref=scat.at[k, :pieces], send_sem=scat_send, recv_sem=scat_recv,
+            device_id=behind(k), device_id_type=MESH,
         ).start()
 
-    acc = scat_own[0] + noise_ref[0] * own_tile
-    pltpu.make_async_copy(scat.at[1:n], scat.at[1:n], scat_recv).wait()
-    acc = acc + jnp.sum(scat[1:n], axis=0)
+    acc = scat_own[0, :pieces] + noise_ref[...].reshape(1, 1) * own_tile[:pieces]
+    pltpu.make_async_copy(scat.at[1:n, :pieces], scat.at[1:n, :pieces], scat_recv).wait()
+    acc = acc + jnp.sum(scat[1:n, :pieces], axis=0)
     for v in range(vecs):
         for c in range(chunks):
             out_ref[0, v : v + 1, LANE * c : LANE * (c + 1)] = acc[v * chunks + c : v * chunks + c + 1]
-    for copy in rate_copies + halo_copies:
-        copy.wait_send()
-    pltpu.make_async_copy(gath.at[1:n], gath.at[1:n], gath_send).wait()
-    pltpu.make_async_copy(scat.at[1:n], scat.at[1:n], scat_send).wait()
+    for copy, target in zip(rate_copies + halo_copies, targets[:2] + targets):
+        pl.when(target)(copy.wait_send)
+    pltpu.make_async_copy(gath.at[1:n, :pieces], gath.at[1:n, :pieces], gath_send).wait()
+    pltpu.make_async_copy(scat.at[1:n, :pieces], scat.at[1:n, :pieces], scat_send).wait()
 
 
 def solution(mesh):
@@ -232,16 +254,14 @@
         dma = pltpu.SemaphoreType.DMA
         return pl.pallas_call(
             functools.partial(kernel_body, n_grp, n_dev),
-            out_shape=jax.ShapeDtypeStruct((own, vecs, nt), F32),
-            in_specs=[
-                pl.BlockSpec(memory_space=vmem),
-                pl.BlockSpec(memory_space=pl.ANY),
-                pl.BlockSpec(memory_space=vmem),
-                pl.BlockSpec(memory_space=smem),
-                pl.BlockSpec(memory_space=smem),
-            ],
+            out_shape=vmem((own, vecs, nt), F32),
+            in_specs=[pl.BlockSpec(memory_space=pl.ANY)] * 5,
             out_specs=pl.BlockSpec(memory_space=vmem),
             scratch_shapes=[
+                vmem(vectors.shape, BF16),
+                vmem(sensor_slot.shape, jnp.int32),
+                vmem(noise_var.shape, F32),
+                smem(smoothing_rate.shape, F32),
                 vmem((sensors, points, nt), BF16),
                 vmem((n, 8, LANE), BF16),
                 vmem((3, 8, LANE), F32),
@@ -251,7 +271,7 @@
                 vmem((n, 8, LANE), F32),
                 vmem((chunks * n, points * LANE), BF16),
                 vmem((points * LANE, chunks * n), BF16),
-                dma, dma, dma, dma((2,)), dma((2,)), dma((4,)), dma((4,)), dma, dma,
+                dma((4,)), dma, dma, dma, dma((2,)), dma((2,)), dma((4,)), dma((4,)), dma, dma,
             ],
             compiler_params=pltpu.CompilerParams(collective_id=0, has_side_effects=True),
         )(vectors, kernel, sensor_slot, noise_var, smoothing_rate)

time: 25.7 us -> 23.1 us (0.90)
  Pallas kernels: 23.6 us -> 21.7 us
  local copies, waits for them, and re-layouts: 1.26 us -> 0.58 us
    pallas_call x1, Pallas kernels: 23.6 us -> 21.7 us  [body(): pl.pallas_call(functools.partial(kernel_body, n_grp, n_dev), out_shape=vm...]
    unnamed x1, local copies, waits for them, and re-layouts: 1.26 us -> 0.58 us
where the time goes in v1:
time: 23.1 us; the launch traced here: 22.9 us
  Pallas kernels  21.7 us (94%)
  between operations  0.66 us (3%)
  local copies, waits for them, and re-layouts  0.58 us (3%)
    pallas_call x1, Pallas kernels, body(): pl.pallas_call(functools.partial(kernel_body, n_grp, n_dev), out_shape=vm...  21.7 us
    unnamed x1, local copies, waits for them, and re-layouts  0.58 us

profile of v1, /device:TPU:0, one launch (start us, length us, event | category | flops | bytes accessed | tf_op | source)
XLA Modules:
  0.0 22.9 jit_solution(8264338108432077424)
XLA Ops:
  0.7 21.7 %shard_map.55 = f32[1,2,384]{2,1,0:T(2,128)S(1)} custom-call(bf16[1,2,384]{2,1,0:T(2,128)(2,1)} %vec_hbm.1, bf16[32,4,384]{2,1,0:T(4,128)(2,1)} %ker_hbm.1, s32[32]{0:T(128)} %slot_hbm.1, f32[1]{0:T(128)S(6)} %copy.8.noise_hbm, f32[4]{0:T(128)} %rate_hbm.1), custom_call_target="tpu_custom_call" | custom-call | tf_op jit(solution)/shard_map/pallas_call | solution.py:255
  22.3 0.6 %copy.7 = f32[1,2,384]{2,1,0:T(2,128)} copy(f32[1,2,384]{2,1,0:T(2,128)S(1)} %shard_map.55) | data formatting | bytes 6144

commit v2 on v1

--- a/solution.py
+++ b/solution.py
@@ -58,23 +58,26 @@
     pieces = vecs * chunks
     grp, dev = lax.axis_index("grp"), lax.axis_index("dev")
 
-    def ahead(k):
-        return ((grp + k // n_dev) % n_grp, (dev + k % n_dev) % n_dev)
-
     def behind(k):
         return ((grp - k // n_dev + n_grp) % n_grp, (dev - k % n_dev + n_dev) % n_dev)
 
-    def slot_of(i):
-        q = i // n_grp
-        along = (n_dev // 2 + (1 - 2 * (q % 2)) * ((q + 1) // 2) + n_dev) % n_dev
-        return (n_grp - 1 - i % n_grp) * n_dev + along
+    def wrapped(i, size):
+        return lax.rem(i + size, size)
+
+    def each_slot(send, sign):
+        for kg in range(n_grp):
+            there = wrapped(grp + sign * kg, n_grp)
+
+            @pl.loop(0 if kg else 1, n_dev, unroll=True)
+            def _(kd, kg=kg, there=there):
+                send(kg * n_dev + kd, (there, wrapped(dev + sign * kd, n_dev)))
 
     gath[...] = jnp.zeros(gath.shape, BF16)
     barrier = pltpu.get_barrier_semaphore()
 
-    @pl.loop(1, n)
-    def _(k):
-        pl.semaphore_signal(barrier, inc=1, device_id=ahead(k), device_id_type=MESH)
+    each_slot(
+        lambda k, device: pl.semaphore_signal(barrier, inc=1, device_id=device, device_id_type=MESH), 1
+    )
 
     loads = [
         pltpu.make_async_copy(source, target, load_sem.at[i])
@@ -99,12 +102,13 @@
     rates[0] = rate
     pl.semaphore_wait(barrier, n - 1)
 
-    @pl.loop(1, n)
-    def _(k):
+    def send_data(k, device):
         pltpu.make_async_remote_copy(
             src_ref=gath.at[0, :pieces], dst_ref=gath.at[k, :pieces], send_sem=gath_send, recv_sem=gath_recv,
-            device_id=ahead(k), device_id_type=MESH,
+            device_id=device, device_id_type=MESH,
         ).start()
+
+    each_slot(send_data, 1)
 
     def beside(offset):
         return (grp, (dev + offset + n_dev) % n_dev)
@@ -223,12 +227,13 @@
                 total = term if total is None else total + term
             scat_own[:, v * chunks + e, :] = total
 
-    @pl.loop(1, n)
-    def _(k):
+    def send_sums(k, device):
         pltpu.make_async_remote_copy(
             src_ref=scat_own.at[k, :pieces], dst_ref=scat.at[k, :pieces], send_sem=scat_send, recv_sem=scat_recv,
-            device_id=behind(k), device_id_type=MESH,
+            device_id=device, device_id_type=MESH,
         ).start()
+
+    each_slot(send_sums, -1)
 
     acc = scat_own[0, :pieces] + noise_ref[...].reshape(1, 1) * own_tile[:pieces]
     pltpu.make_async_copy(scat.at[1:n, :pieces], scat.at[1:n, :pieces], scat_recv).wait()

time: 23.1 us -> 22.8 us (0.987)
  Pallas kernels: 21.7 us -> 21.4 us
    pallas_call x1, Pallas kernels: 21.7 us -> 21.4 us  [body(): pl.pallas_call(functools.partial(kernel_body, n_grp, n_dev), out_shape=vm...]
where the time goes in v2:
time: 22.8 us; the launch traced here: 22.6 us
  Pallas kernels  21.4 us (94%)
  between operations  0.66 us (3%)
  local copies, waits for them, and re-layouts  0.58 us (3%)
    pallas_call x1, Pallas kernels, body(): pl.pallas_call(functools.partial(kernel_body, n_grp, n_dev), out_shape=vm...  21.4 us
    unnamed x1, local copies, waits for them, and re-layouts  0.58 us

profile of v2, /device:TPU:0, one launch (start us, length us, event | category | flops | bytes accessed | tf_op | source)
XLA Modules:
  0.0 22.6 jit_solution(16269884362442731813)
XLA Ops:
  0.7 21.4 %shard_map.55 = f32[1,2,384]{2,1,0:T(2,128)S(1)} custom-call(bf16[1,2,384]{2,1,0:T(2,128)(2,1)} %vec_hbm.1, bf16[32,4,384]{2,1,0:T(4,128)(2,1)} %ker_hbm.1, s32[32]{0:T(128)} %slot_hbm.1, f32[1]{0:T(128)S(6)} %copy.8.noise_hbm, f32[4]{0:T(128)} %rate_hbm.1), custom_call_target="tpu_custom_call" | custom-call | tf_op jit(solution)/shard_map/pallas_call | solution.py:260
  22.1 0.6 %copy.7 = f32[1,2,384]{2,1,0:T(2,128)} copy(f32[1,2,384]{2,1,0:T(2,128)S(1)} %shard_map.55) | data formatting | bytes 6144
